TPU v7x, 32 devices: a whole 2x2x4 slice. The times are simulated.
32 devices in a mesh: expert: 8 (over z, y), layer: 4 (over x, core).
Axes of the slice: x: 2, y: 2, z: 4, core: 2. Of those that a mesh axis runs over, the one named last changes fastest.
Arguments:
- gradient: bfloat16 [32, 16, 1536], P(('layer', 'expert')), parts along dimension 0, may hold values from -80 to 80
- prior_stat: float32 [32, 8], P('layer'), parts along dimension 0, may hold values from -600 to 600, as said below
Outputs:
- update: bfloat16 [32, 16, 1536], P(('layer', 'expert')), parts along dimension 0
- statistic: float32 [32, 8], P('layer'), parts along dimension 0
There are 4 independent parts, one for each index of `layer`. A program takes and returns all parts, laid end to end along the dimension named above; each array names one. Nothing has to cross between parts.
Inputs may be any that keep to these rules, and one draw needn't show every extreme that they name: `prior_stat`: symmetric positive definite.
All inputs are finite; a program needn't handle non-finite values.
Results may differ from a plain program's by a relative error of at most 0.001.
The roundings to bfloat16 on the way count: a program that leaves them out, or rounds other values in their place, can miss the bound.
Values may be sent and summed in bfloat16 or wider, within the bound.
A program may use at most 64 MiB of HBM per device.

v0:
```python
import jax
import jax.numpy as jnp
from jax import lax
from jax.sharding import PartitionSpec as P

ITERS = 5
ridge_rate = 0.001
energy_floor = 1e-06


def matmul_high(left, right):
    return jnp.dot(left, right, precision=lax.Precision.HIGHEST, preferred_element_type=jnp.float32)


def inverse_root(statistic):
    count_rows = statistic.shape[0]
    identity = jnp.eye(count_rows, dtype=jnp.float32)
    ridge_term = ridge_rate * jnp.trace(statistic) / count_rows
    shifted = statistic + ridge_term * identity
    start_scale = 2.5 / jnp.sqrt(jnp.sum(shifted * shifted))
    matrix = start_scale * shifted
    root = start_scale**0.25 * identity
    for repeat in range(ITERS):
        factor = 1.25 * identity - 0.25 * matrix
        root = matmul_high(root, factor)
        square = matmul_high(factor, factor)
        matrix = matmul_high(matmul_high(square, square), matrix)
    return root


def apply_graft(mixed_bf, graft):
    fenced = lax.optimization_barrier(mixed_bf)
    return (graft * fenced.astype(jnp.float32)).astype(jnp.bfloat16)


def slice_grams(pieces):
    grams = jnp.einsum("eqrf,gqrf->eqrg", pieces, pieces, preferred_element_type=jnp.float32)
    return (pieces, grams)


def body(gradient, prior_stat):
    experts = prior_stat.shape[0]
    owners = lax.axis_size("expert")
    local_experts = gradient.shape[0]
    slab_rows = gradient.shape[1]
    width = gradient.shape[2]
    entry_count = slab_rows * width
    slice_rows = slab_rows // owners
    blocked = gradient.reshape(local_experts, owners, slice_rows, width)
    regrouped, row_grams = slice_grams(
        lax.all_to_all(blocked, "expert", split_axis=1, concat_axis=0, tiled=True)
    )
    summed = lax.psum(jnp.sum(row_grams, axis=(1, 2)), "expert")
    gram_mean = summed / entry_count
    statistic = prior_stat + gram_mean
    root_bf = inverse_root(statistic).astype(jnp.bfloat16)
    flattened = regrouped.reshape(experts, -1)
    products = jnp.dot(root_bf, flattened, preferred_element_type=jnp.float32)
    mixed_bf = products.astype(jnp.bfloat16).reshape(experts, slice_rows, width)
    root_wide = root_bf.astype(jnp.float32)
    update_energy = jnp.sum(matmul_high(root_wide, gram_mean) * root_wide) / experts
    grad_energy = jnp.trace(gram_mean) / experts
    graft = jnp.sqrt((grad_energy + energy_floor) / (update_energy + energy_floor))
    grafted = apply_graft(mixed_bf, graft)
    update = lax.all_to_all(grafted, "expert", split_axis=0, concat_axis=1, tiled=True)
    return (update, statistic)


def solution(mesh):
    placed = (P(("layer", "expert"), None, None), P("layer", None))
    return jax.shard_map(
        body,
        mesh=mesh,
        in_specs=placed,
        out_specs=(P(("layer", "expert"), None, None), P("layer", None)),
        check_vma=False,
    )
```

profile of v0, /device:TPU:0, one launch (start us, length us, event | category | flops | bytes accessed | tf_op | source)
XLA Modules:
  0.0 50.7 jit_solution(7048645987614553434)
XLA Ops:
  0.6 0.8 %reshape.28 = bf16[1,8,2,1536]{3,2,1,0:T(2,128)(2,1)S(1)} reshape(bf16[1,16,1536]{2,1,0:T(8,128)(2,1)} %param.2) | data formatting | bytes 98304 | tf_op jit(solution)/shard_map/reshape | solution.py:49
  1.5 13.9 %all_to_all.21 = bf16[1,8,2,1536]{3,2,0,1:T(2,128)(2,1)S(1)} all-to-all(bf16[1,8,2,1536]{3,2,0,1:T(2,128)(2,1)S(1)} %bitcast.37), channel_id=1, replica_groups=mesh['expert'=8,'layer'=4] {'expert'}, dimensions={1} | all-to-all | bytes 98304 | tf_op jit(solution)/shard_map/all_to_all | solution.py:51
  15.5 18.0 %psum.7 = f32[8,8]{1,0:T(8,128)S(1)} all-reduce(f32[8,8]{1,0:T(8,128)S(1)} %convolution_bitcast_fusion), channel_id=1, replica_groups=mesh['expert'=8,'layer'=4] {'expert'}, use_global_device_ids=true, to_apply=%region_0.0 | all-reduce | flops 64 | bytes 512 | tf_op jit(solution)/shard_map/psum | solution.py:53
  33.5 0.7 %select_reduce_fusion = (f32[]{:T(128)}, f32[8,8]{1,0:T(8,128)S(1)}, f32[]{:T(128)}) fusion(f32[8,8]{1,0:T(8,128)S(1)} %copy-done.1, f32[8,8]{1,0:T(8,128)S(1)} %psum.7), kind=kLoop, calls=%fused_computation.18 | loop fusion | flops 446 | bytes 776 | tf_op jit(solution)/shard_map/jit(trace)/reduce_sum | solution.py:18
  34.8 0.6 %multiply_reduce_fusion = f32[]{:T(128)} fusion(f32[8,8]{1,0:T(8,128)S(1)} %get-tuple-element.3, f32[]{:T(128)S(6)} %div.24), kind=kLoop, calls=%fused_computation.16 | loop fusion | flops 319 | bytes 264 | tf_op jit(solution)/shard_map/reduce_sum | solution.py:20
  36.1 0.1 fusion.15
  36.5 0.1 fusion.71
  36.6 0.1 fusion.6
  36.7 0.1 fusion.9
  36.9 0.1 fusion.10
  37.0 0.1 fusion.72
  37.1 0.1 fusion.73
  37.3 0.1 fusion.11
  37.4 0.1 fusion.12
  37.5 0.1 fusion.74
  37.7 0.1 fusion.75
  37.8 0.1 fusion.13
  38.0 0.1 fusion.14
  38.1 0.1 fusion.76
  38.2 0.1 fusion
  38.4 0.1 convolution_convert_fusion.1
  38.5 0.7 %fusion.1 = f32[]{:T(128)} fusion(bf16[8,8]{1,0:T(8,128)(2,1)S(1)} %convolution_convert_fusion.1, f32[8,8]{1,0:T(8,128)S(1)} %psum.7), kind=kOutput, calls=%fused_computation.6 | convolution fusion | flops 6399 | bytes 388 | tf_op jit(solution)/shard_map/dot_general | solution.py:12
  40.9 9.2 %all_to_all.22 = bf16[8,2,1536]{2,1,0:T(2,128)(2,1)S(1)} all-to-all(bf16[8,2,1536]{2,1,0:T(2,128)(2,1)S(1)} %copy.12), channel_id=1, replica_groups=mesh['expert'=8,'layer'=4] {'expert'}, dimensions={0} | all-to-all | bytes 98304 | tf_op jit(solution)/shard_map/all_to_all | solution.py:65
  50.1 0.6 %all_to_all.8 = bf16[1,16,1536]{2,1,0:T(8,128)(2,1)} reshape(bf16[8,2,1536]{2,1,0:T(2,128)(2,1)S(1)} %all_to_all.22) | data formatting | bytes 98304 | tf_op jit(solution)/shard_map/all_to_all | solution.py:65
  (10 shorter events, 0.5 us)
Async XLA Ops:
  15.5 18.0 %copy-start.1 = (f32[8,8]{1,0:T(8,128)S(1)}, f32[8,8]{1,0:T(8,128)}, u32[]{:S(2)}) copy-start(f32[8,8]{1,0:T(8,128)} %param.3) | copy-start | bytes 772
  34.2 2.4 %copy-start = (f32[8,8]{1,0:T(8,128)}, f32[8,8]{1,0:T(8,128)S(1)}, u32[]{:S(2)}) copy-start(f32[8,8]{1,0:T(8,128)S(1)} %get-tuple-element.3) | copy-start | bytes 772
where the time goes:
time: 51 us; the launch traced here: 50.7 us
  blocking collectives  41.1 us (81%)
  between operations  3.51 us (7%)
  matrix products  3.31 us (6%)
  local copies, waits for them, and re-layouts  1.52 us (3%)
  other arithmetic  1.3 us (3%)
    psum x1, blocking collectives, body(): summed = lax.psum(jnp.sum(row_grams, axis=(1, 2)), 'expert')  18 us
    all_to_all x1, blocking collectives, body(): lax.all_to_all(blocked, 'expert', split_axis=1, concat_axis=0, tiled=True)  13.9 us
    all_to_all x1, blocking collectives, body(): lax.all_to_all(grafted, 'expert', split_axis=0, concat_axis=1, tiled=True)  9.17 us
    dot_general x18, matrix products, matmul_high(): jnp.dot(left, right, precision=lax.Precision.HIGHEST, preferred_element_t...  3.05 us

commit v1 on v0

--- a/solution.py
+++ b/solution.py
@@ -6,6 +6,11 @@
 ITERS = 5
 ridge_rate = 0.001
 energy_floor = 1e-06
+
+
+def gather_and_add(block, mesh_axis):
+    parts = lax.all_gather(block, mesh_axis)
+    return jnp.sum(parts, axis=0)
 
 
 def matmul_high(left, right):
@@ -50,7 +55,7 @@
     regrouped, row_grams = slice_grams(
         lax.all_to_all(blocked, "expert", split_axis=1, concat_axis=0, tiled=True)
     )
-    summed = lax.psum(jnp.sum(row_grams, axis=(1, 2)), "expert")
+    summed = gather_and_add(jnp.sum(row_grams, axis=(1, 2)), "expert")
     gram_mean = summed / entry_count
     statistic = prior_stat + gram_mean
     root_bf = inverse_root(statistic).astype(jnp.bfloat16)

time: 51 us -> 64.3 us (1.26)
  blocking collectives: 41.1 us -> 53.7 us
  local copies, waits for them, and re-layouts: 1.52 us -> 2.19 us
    all_gather x0 -> x1, blocking collectives: none -> 30.6 us  [gather_and_add(): parts = lax.all_gather(block, mesh_axis)]
    psum x1 -> x0, blocking collectives: 18 us -> none  [body(): summed = lax.psum(jnp.sum(row_grams, axis=(1, 2)), 'expert')]
    unnamed x5, local copies, waits for them, and re-layouts: 0.02 us -> 0.69 us
where the time goes in v1:
time: 64.3 us; the launch traced here: 64 us
  blocking collectives  53.7 us (84%)
  between operations  3.51 us (5%)
  matrix products  3.31 us (5%)
  local copies, waits for them, and re-layouts  2.19 us (3%)
  other arithmetic  1.31 us (2%)
    all_gather x1, blocking collectives, gather_and_add(): parts = lax.all_gather(block, mesh_axis)  30.6 us
    all_to_all x1, blocking collectives, body(): lax.all_to_all(blocked, 'expert', split_axis=1, concat_axis=0, tiled=True)  13.9 us
    all_to_all x1, blocking collectives, body(): lax.all_to_all(grafted, 'expert', split_axis=0, concat_axis=1, tiled=True)  9.17 us
    dot_general x18, matrix products, matmul_high(): jnp.dot(left, right, precision=lax.Precision.HIGHEST, preferred_element_t...  3.05 us

profile of v1, /device:TPU:0, one launch (start us, length us, event | category | flops | bytes accessed | tf_op | source)
XLA Modules:
  0.0 64.0 jit_solution(16664513255025962189)
XLA Ops:
  0.6 0.8 %reshape.28 = bf16[1,8,2,1536]{3,2,1,0:T(2,128)(2,1)S(1)} reshape(bf16[1,16,1536]{2,1,0:T(8,128)(2,1)} %param.2) | data formatting | bytes 98304 | tf_op jit(solution)/shard_map/reshape | solution.py:54
  1.5 13.9 %all_to_all.21 = bf16[1,8,2,1536]{3,2,0,1:T(2,128)(2,1)S(1)} all-to-all(bf16[1,8,2,1536]{3,2,0,1:T(2,128)(2,1)S(1)} %bitcast.39), channel_id=1, replica_groups=mesh['expert'=8,'layer'=4] {'expert'}, dimensions={1} | all-to-all | bytes 98304 | tf_op jit(solution)/shard_map/all_to_all | solution.py:56
  15.5 30.6 %all-gather = f32[64,8]{1,0:T(8,128)S(1)} all-gather(f32[8,8]{1,0:T(8,128)S(1)} %convolution_bitcast_fusion), channel_id=2, replica_groups=mesh['expert'=8,'layer'=4] {'expert'}, dimensions={0}, use_global_device_ids=true | all-gather | bytes 2304 | tf_op jit(solution)/shard_map/all_gather | solution.py:12
  46.1 0.7 %copy-done.1 = f32[8,8]{1,0:T(8,128)S(1)} copy-done((f32[8,8]{1,0:T(8,128)S(1)}, f32[8,8]{1,0:T(8,128)}, u32[]{:S(2)}) %copy-start.1) | copy-done | bytes 280
  46.8 0.7 %select_reduce_fusion = (f32[]{:T(128)}, f32[8,8]{1,0:T(8,128)S(1)}, f32[]{:T(128)}) fusion(f32[8,8]{1,0:T(8,128)S(1)} %copy-done.1, f32[8,8]{1,0:T(8,128)S(1)} %bitcast_reduce_fusion), kind=kLoop, calls=%fused_computation.19 | loop fusion | flops 446 | bytes 776 | tf_op jit(solution)/shard_map/jit(trace)/reduce_sum | solution.py:23
  48.1 0.6 multiply_reduce_fusion
  49.4 0.1 fusion.15
  49.9 0.1 fusion.6
  50.0 0.1 fusion.9
  50.2 0.1 fusion.10
  50.3 0.1 fusion.72
  50.4 0.1 fusion.73
  50.6 0.1 fusion.11
  50.7 0.1 fusion.12
  50.8 0.1 fusion.74
  51.0 0.1 fusion.75
  51.1 0.1 fusion.13
  51.3 0.1 fusion.14
  51.4 0.1 fusion.76
  51.5 0.1 fusion
  51.7 0.1 convolution_convert_fusion.1
  51.8 0.7 %fusion.1 = f32[]{:T(128)} fusion(bf16[8,8]{1,0:T(8,128)(2,1)S(1)} %convolution_convert_fusion.1, f32[8,8]{1,0:T(8,128)S(1)} %bitcast_reduce_fusion), kind=kOutput, calls=%fused_computation.6 | convolution fusion | flops 6399 | bytes 388 | tf_op jit(solution)/shard_map/dot_general | solution.py:17
  54.2 9.2 %all_to_all.22 = bf16[8,2,1536]{2,1,0:T(2,128)(2,1)S(1)} all-to-all(bf16[8,2,1536]{2,1,0:T(2,128)(2,1)S(1)} %copy.12), channel_id=1, replica_groups=mesh['expert'=8,'layer'=4] {'expert'}, dimensions={0} | all-to-all | bytes 98304 | tf_op jit(solution)/shard_map/all_to_all | solution.py:70
  63.4 0.6 %all_to_all.8 = bf16[1,16,1536]{2,1,0:T(8,128)(2,1)} reshape(bf16[8,2,1536]{2,1,0:T(2,128)(2,1)S(1)} %all_to_all.22) | data formatting | bytes 98304 | tf_op jit(solution)/shard_map/all_to_all | solution.py:70
  (11 shorter events, 0.6 us)
Async XLA Ops:
  46.1 0.7 %copy-start.1 = (f32[8,8]{1,0:T(8,128)S(1)}, f32[8,8]{1,0:T(8,128)}, u32[]{:S(2)}) copy-start(f32[8,8]{1,0:T(8,128)} %param.3) | copy-start | bytes 772
  47.5 2.4 %copy-start = (f32[8,8]{1,0:T(8,128)}, f32[8,8]{1,0:T(8,128)S(1)}, u32[]{:S(2)}) copy-start(f32[8,8]{1,0:T(8,128)S(1)} %get-tuple-element.3) | copy-start | bytes 772
